TPU v7x, 512 devices: a whole 4x8x8 slice. The times are simulated.
512 devices in a mesh: dp: 4 (over x_hi, core), context: 16 (over x_lo, z), tensor: 8 (over y).
Axes of the slice: x: 4 (x_hi: 2, x_lo: 2; x = x_hi * 2 + x_lo), y: 8, z: 8, core: 2. Of those that a mesh axis runs over, the one named last changes fastest.
Arguments:
- tokens: bfloat16 [32768, 4096], P(('dp', 'context', 'tensor')), parts along dimension 0, may hold values from -6 to 6
- norm_gain: bfloat16 [4096], replicated, may hold values from 0.099609375 to 1.8984375
- w_query: bfloat16 [4096, 2048], P(None, 'tensor'), may hold values from -2.03125 to 2.03125
- key_matrix: bfloat16 [4096, 1024], P(None, 'tensor'), may hold values from -0.109375 to 0.109375
- value_matrix: bfloat16 [4096, 1024], P(None, 'tensor'), may hold values from -0.09375 to 0.09375
- seg_ids: int32 [32768], P('dp'), parts along dimension 0, may hold values from 0 to 7, never falling along the last dimension, each value on 1 to 4096 neighbouring positions
Outputs:
- attended: bfloat16 [32768, 2048], P(('dp', 'context'), 'tensor'), parts along dimension 0
There are 4 independent parts, one for each index of `dp`. A program takes and returns all parts, laid end to end along the dimension named above; an argument that names none is the same for every part. Nothing has to cross between parts.
Inputs may be any that keep to these rules, and one draw needn't show every extreme that they name: `seg_ids`: never falls along the row; each of the 8 documents covers 1 to 4096 positions, one exactly 4096.
All inputs are finite; a program needn't handle non-finite values.
Results may differ from a plain program's by a relative error of at most 0.0078.
Values may be sent and summed in bfloat16 or wider, within the bound.
A program may use at most 64 MiB of HBM per device.

v0:
```python
import math
import jax
import jax.numpy as jnp
from jax import lax
from jax.sharding import PartitionSpec as P

HEAD_SIZE = 128


def sent_together(arrays, axis, dim, along):
    widths = [a.shape[along] for a in arrays]
    both = jnp.concatenate(arrays, axis=along)
    filled = lax.all_gather(both, axis, axis=dim, tiled=True)
    return tuple(jnp.split(filled, [sum(widths[:k]) for k in range(1, len(widths))], axis=along))


def rotate(vectors, positions):
    half_width = vectors.shape[-1] // 2
    inv_freq = jnp.exp(
        -(jnp.arange(half_width, dtype=jnp.float32) * (2.0 / vectors.shape[-1]))
        * math.log(500000.0)
    )
    angles = positions.astype(jnp.float32)[:, None] * inv_freq[None, :]
    cosine = jnp.cos(angles)[:, None, :]
    sine = jnp.sin(angles)[:, None, :]
    front_half = vectors[..., :half_width]
    back_half = vectors[..., half_width:]
    return jnp.concatenate(
        [front_half * cosine - back_half * sine, back_half * cosine + front_half * sine], -1
    )


def merge_block(
    states_in, query_heads, query_pos, query_segs, key_part, val_part, key_segs, key_pos
):
    peak_old, totals, weighted = states_in
    scores = jnp.einsum(
        "qkgd,skd->kgqs", query_heads, key_part, preferred_element_type=jnp.float32
    ) * (1.0 / math.sqrt(HEAD_SIZE))
    visible = (key_pos[None, :] <= query_pos[:, None]) & (key_segs[None, :] == query_segs[:, None])
    scores = jnp.where(visible[None, None], scores, -1e30)
    peak_new = jnp.maximum(peak_old, jnp.max(scores, -1))
    probs = jnp.where(visible[None, None], jnp.exp(scores - peak_new[..., None]), 0.0)
    rescale = jnp.exp(peak_old - peak_new)
    totals = totals * rescale + jnp.sum(probs, -1)
    weighted = weighted * rescale[..., None] + jnp.einsum(
        "kgqs,skd->kgqd", probs.astype(jnp.bfloat16), val_part, preferred_element_type=jnp.float32
    )
    return (peak_new, totals, weighted)


def body(tokens, norm_gain, w_query, key_matrix, value_matrix, seg_ids):
    wide_tokens = tokens.astype(jnp.float32)
    rms_normalized = (
        wide_tokens
        * lax.rsqrt(jnp.mean(wide_tokens * wide_tokens, -1, keepdims=True) + 1e-05)
        * norm_gain.astype(jnp.float32)
    ).astype(jnp.bfloat16)
    pieces = lax.all_gather(rms_normalized, "tensor", axis=0, tiled=True)
    projected = jnp.concatenate(
        [
            jnp.dot(pieces, w_query, preferred_element_type=jnp.float32),
            jnp.dot(pieces, key_matrix, preferred_element_type=jnp.float32),
            jnp.dot(pieces, value_matrix, preferred_element_type=jnp.float32),
        ],
        1,
    )
    span_rows = projected.shape[0]
    width_q = w_query.shape[1]
    width_k = key_matrix.shape[1]
    heads_q = width_q // HEAD_SIZE
    heads_kv = width_k // HEAD_SIZE
    heads_per_group = heads_q // heads_kv
    offset = lax.axis_index("context") * span_rows
    positions = offset + jnp.arange(span_rows, dtype=jnp.int32)
    query = rotate(projected[:, :width_q].reshape(span_rows, heads_q, HEAD_SIZE), positions).astype(
        jnp.bfloat16
    )
    key = rotate(
        projected[:, width_q : width_q + width_k].reshape(span_rows, heads_kv, HEAD_SIZE), positions
    ).astype(jnp.bfloat16)
    key = key.reshape(span_rows, width_k)
    value_rows = projected[:, width_q + width_k :].astype(jnp.bfloat16)
    groups = (query, positions, lax.dynamic_slice_in_dim(seg_ids, offset, span_rows, 0))
    query_rows, query_pos, query_segs = groups
    count = query_rows.shape[0]
    prepared = [
        (query_rows.reshape(count, heads_kv, heads_per_group, HEAD_SIZE), query_pos, query_segs)
    ]
    initial = [
        (
            jnp.full((heads_kv, heads_per_group, count), -1e30, jnp.float32),
            jnp.zeros((heads_kv, heads_per_group, count), jnp.float32),
            jnp.zeros((heads_kv, heads_per_group, count, HEAD_SIZE), jnp.float32),
        )
    ]
    states = tuple(initial)
    anchor = jnp.int32(0)
    keys_in, values_in = sent_together((key, value_rows), "context", 0, 1)
    length = keys_in.shape[0]
    sub_rows = math.gcd(length, 512)
    parts_count = length // sub_rows
    key_blocks = keys_in.reshape(parts_count, sub_rows, heads_kv, HEAD_SIZE)
    value_blocks = values_in.reshape(parts_count, sub_rows, heads_kv, HEAD_SIZE)
    key_pos_all = jnp.arange(length, dtype=jnp.int32)
    seg_blocks = seg_ids.reshape(parts_count, sub_rows)
    pos_blocks = key_pos_all.reshape(parts_count, sub_rows)
    results = []
    for (query_heads, query_pos, query_segs), states_in in zip(prepared, states):
        skipped = (anchor > jnp.max(query_pos)) | (seg_ids[length - 1] < jnp.min(query_segs))

        def update(carried, query_heads=query_heads, query_pos=query_pos, query_segs=query_segs):

            def inner(running, slices):
                key_part, val_part, key_segs, key_pos = slices
                return (
                    merge_block(
                        running,
                        query_heads,
                        query_pos,
                        query_segs,
                        key_part,
                        val_part,
                        key_segs,
                        key_pos,
                    ),
                    None,
                )

            return lax.scan(inner, carried, (key_blocks, value_blocks, seg_blocks, pos_blocks))[0]

        results.append(lax.cond(skipped, lambda carried: carried, update, states_in))
    finals = tuple(results)
    outputs = []
    for peak_val, totals, weighted in finals:
        count = weighted.shape[2]
        normalized = weighted / totals[..., None]
        outputs.append(
            jnp.transpose(normalized, (2, 0, 1, 3)).reshape(count, width_q).astype(jnp.bfloat16)
        )
    return outputs[0]


def solution(mesh):
    in_specs = (
        P(("dp", "context", "tensor"), None),
        P(),
        P(None, "tensor"),
        P(None, "tensor"),
        P(None, "tensor"),
        P("dp"),
    )
    out_specs = P(("dp", "context"), "tensor")
    return jax.shard_map(body, mesh=mesh, in_specs=in_specs, out_specs=out_specs, check_vma=False)
```

profile of v0, /device:TPU:8, one launch (start us, length us, event | category | flops | bytes accessed | tf_op | source)
XLA Modules:
  0.0 281.3 jit_solution(2508843274565658553)
XLA Ops:
  6.5 0.8 convert_element_type.49
  7.4 1.2 fusion.23
  8.6 2.0 fusion.25
  10.8 60.4 %all-gather.3.cloned.1.call-done = bf16[512,4096]{1,0:T(8,128)(2,1)} async-done(((bf16[64,4096]{1,0:T(8,128)(2,1)}), bf16[512,4096]{1,0:T(8,128)(2,1)}) %all-gather.3.cloned.1.call-update) | async-done | bytes 4194320 | tf_op jit(solution)/shard_map/all_gather | solution.py:59
  71.2 4.1 %convolution_bitcast_fusion.1 = f32[512,1,128]{0,2,1:T(8,128)S(1)} fusion(bf16[512,4096]{1,0:T(8,128)(2,1)} %all-gather.3.cloned.1.call-done, bf16[4096,128]{1,0:T(8,128)(2,1)} %param.13), kind=kOutput, calls=%fused_computation.37 | convolution fusion | flops 536870912 | bytes 5505024 | tf_op jit(solution)/shard_map/dot_general | solution.py:63
  75.9 1.5 convolution_convert_fusion
  77.5 0.7 pad_maximum_fusion
  78.2 0.7 fusion.40
  78.9 0.6 slice.15
  80.2 0.8 fusion.41
  82.3 1.8 multiply_cosine_fusion
  84.1 3.5 %fusion.44 = f32[512,256]{0,1:T(8,128)S(1)} fusion(bf16[512,4096]{1,0:T(8,128)(2,1)} %all-gather.3.cloned.1.call-done, bf16[4096,256]{1,0:T(8,128)(2,1)S(1)} %copy-done), kind=kOutput, calls=%fused_computation.73 | convolution fusion | flops 1073741824 | bytes 6815744 | tf_op jit(solution)/shard_map/dot_general | solution.py:62
  88.1 1.2 fusion.26
  89.4 69.8 %all-gather.5.cloned.1.call-done = bf16[8192,256]{0,1:T(8,128)(2,1)} async-done(((bf16[512,256]{0,1:T(8,128)(2,1)}), bf16[8192,256]{0,1:T(8,128)(2,1)}) %all-gather.5.cloned.1.call-update) | async-done | bytes 4194320 | tf_op jit(solution)/shard_map/all_gather | solution.py:13
  159.2 114.0 %conditional.1 = (f32[1,2,512]{2,1,0:T(2,128)S(1)}, f32[1,2,512,128]{3,2,1,0:T(8,128)S(1)}) conditional(s32[]{:T(128)} %convert_element_type.47, (bf16[8192,256]{0,1:T(8,128)(2,1)}, s32[8192]{0:T(1024)S(1)}, s32[16,512]{1,0:T(8,128)S(1)}, s32[16,512]{1,0:T(8,128)S(1)}, s32[512]{0:T(512)S(1)}, /*index=5*/s32[512]{0:T(512)S(1)}, ...), branch_computations={%region_3.8_spmd, %region_8.9_spmd} | conditional | flops 276453376 | bytes 34325800 | solution.py:132
  159.2 6.4 %copy.10 = bf16[8192,256]{1,0:T(8,128)(2,1)} copy(bf16[8192,256]{0,1:T(8,128)(2,1)} %get-tuple-element.134) | data formatting | bytes 8388608 | tf_op jit(solution)/shard_map
  165.6 4.5 %fusion.42 = (bf16[8192,128]{1,0:T(8,128)(2,1)}, bf16[8192,128]{1,0:T(8,128)(2,1)}) fusion(bf16[8192,256]{1,0:T(8,128)(2,1)} %copy.10), kind=kLoop, calls=%fused_computation.71 | loop fusion | bytes 8388608 | tf_op jit(solution)/shard_map/split | solution.py:14
  170.1 103.1 %while.14 = (s32[]{:T(128)}, f32[1,2,512]{2,1,0:T(2,128)S(1)}, f32[1,2,512]{2,1,0:T(2,128)S(1)}, f32[1,2,512,128]{3,2,1,0:T(8,128)S(1)}, s32[16,512]{1,0:T(8,128...) while((s32[]{:T(128)}, f32[1,2,512]{2,1,0:T(2,128)S(1)}, ...), condition=%wide.region_7.7_spmd.clone, body=%wide.region_4.6_spmd.clone.sunk | while | flops 276436992 | bytes 17384616 | solution.py:130
  170.4 2.8 fusion.59
  173.2 2.7 fusion.62
  176.0 0.6 fusion.61
  176.9 2.8 fusion.59
  179.7 2.7 fusion.62
  182.4 0.6 fusion.61
  183.3 2.8 fusion.59
  186.1 2.7 fusion.62
  188.8 0.6 fusion.61
  189.8 2.8 fusion.59
  192.6 2.7 fusion.62
  195.3 0.6 fusion.61
  196.2 2.8 fusion.59
  199.0 2.7 fusion.62
  201.7 0.6 fusion.61
  202.6 2.8 fusion.59
  205.4 2.7 fusion.62
  208.2 0.6 fusion.61
  209.1 2.8 fusion.59
  211.9 2.7 fusion.62
  214.6 0.6 fusion.61
  215.5 2.8 fusion.59
  218.3 2.7 fusion.62
  221.1 0.6 fusion.61
  222.0 2.8 fusion.59
  224.8 2.7 fusion.62
  227.5 0.6 fusion.61
  228.4 2.8 fusion.59
  231.2 2.7 fusion.62
  233.9 0.6 fusion.61
  234.9 2.8 fusion.59
  237.7 2.7 fusion.62
  240.4 0.6 fusion.61
  241.3 2.8 fusion.59
  244.1 2.7 fusion.62
  246.8 0.6 fusion.61
  247.7 2.8 fusion.59
  250.5 2.7 fusion.62
  253.3 0.6 fusion.61
  254.2 2.8 fusion.59
  257.0 2.7 fusion.62
  260.6 2.8 fusion.59
  263.4 2.7 fusion.62
  267.1 2.8 fusion.59
  269.9 2.7 fusion.62
  273.7 0.7 copy.17
  (145 shorter events, 8.7 us)
Async XLA Ops:
  6.5 77.6 %copy-start = (bf16[4096,256]{1,0:T(8,128)(2,1)S(1)}, bf16[4096,256]{1,0:T(8,128)(2,1)}, u32[]{:S(2)}) copy-start(bf16[4096,256]{1,0:T(8,128)(2,1)} %param.12) | copy-start | bytes 6291460
  6.5 64.7 %all-gather.3.cloned.1.call-start = ((), (), s32[]{:S(2)}) async-start(), calls=%async_computation | async-start | bytes 4718592 | tf_op jit(solution)/shard_map/all_gather | solution.py:59
  10.7 148.5 %all-gather.5.cloned.1.call-start = ((), (), s32[]{:S(2)}) async-start(), calls=%async_computation.1 | async-start | bytes 4456448 | tf_op jit(solution)/shard_map/all_gather | solution.py:13
  10.8 65.1 %copy-start.3 = (bf16[4096,128]{1,0:T(8,128)(2,1)S(1)}, bf16[4096,128]{1,0:T(8,128)(2,1)}, u32[]{:S(2)}) copy-start(bf16[4096,128]{1,0:T(8,128)(2,1)} %param.14) | copy-start | bytes 3145732
  71.2 4.7 %copy-start.2 = (bf16[512,4096]{1,0:T(8,128)(2,1)S(1)}, bf16[512,4096]{1,0:T(8,128)(2,1)}, u32[]{:S(2)}) copy-start(bf16[512,4096]{1,0:T(8,128)(2,1)} %all-gather.3.cloned.1.call-done) | copy-start | bytes 12582916
  75.9 3.0 %copy-start.4 = (s32[8192]{0:T(1024)S(1)}, s32[8192]{0:T(1024)}, u32[]{:S(2)}) copy-start(s32[8192]{0:T(1024)} %param.15) | copy-start | bytes 98308
  173.2 2.7 copy-start.1
  179.7 2.7 copy-start.1
  186.1 2.7 copy-start.1
  192.6 2.7 copy-start.1
  199.0 2.7 copy-start.1
  205.4 2.7 copy-start.1
  211.9 2.7 copy-start.1
  218.3 2.7 copy-start.1
  224.8 2.7 copy-start.1
  231.2 2.7 copy-start.1
  237.6 2.7 copy-start.1
  244.1 2.7 copy-start.1
  250.5 2.7 copy-start.1
  257.0 2.7 copy-start.1
  263.4 2.7 copy-start.1
  269.9 2.7 copy-start.1
Sparse Core Ops, SparseCore 0:
  10.8 60.3 all-gather.2
  78.3 80.8 all-gather.4
where the time goes:
time: 282 us; the launch traced here: 281 us
  waiting for transfers between devices  130 us (46%)
  matrix products  96.7 us (34%)
  other arithmetic  24.4 us (9%)
  between operations  15.6 us (6%)
  local copies, waits for them, and re-layouts  13.3 us (5%)
    all_gather x1, waiting for transfers between devices, sent_together(): filled = lax.all_gather(both, axis, axis=dim, tiled=True)  69.8 us
    all_gather x1, waiting for transfers between devices, body(): pieces = lax.all_gather(rms_normalized, 'tensor', axis=0, tiled=True)  60.4 us
    dot_general x16, matrix products, merge_block(): jnp.einsum('qkgd,skd->kgqs', query_heads, key_part, preferred_element_typ...  44.4 us
    dot_general x16, matrix products, merge_block(): jnp.einsum('kgqs,skd->kgqd', probs.astype(jnp.bfloat16), val_part, prefer...  43.2 us
    reduce_sum x16, other arithmetic, merge_block(): totals = totals * rescale + jnp.sum(probs, -1)  9.2 us
    another operation x1, local copies, waits for them, and re-layouts  6.43 us
  transfers between devices with their start and end apart: 2, of which 2 were waited for; matrix products, arithmetic and copies ran while one was open for 3% of the time, Pallas kernels for 0%

commit v1 on v0

--- a/solution.py
+++ b/solution.py
@@ -56,7 +56,24 @@
         * lax.rsqrt(jnp.mean(wide_tokens * wide_tokens, -1, keepdims=True) + 1e-05)
         * norm_gain.astype(jnp.float32)
     ).astype(jnp.bfloat16)
-    pieces = lax.all_gather(rms_normalized, "tensor", axis=0, tiled=True)
+    ways, here, step = (lax.axis_size("tensor"), lax.axis_index("tensor"), rms_normalized.shape[0])
+    shape = [n * ways if d == 0 else n for d, n in enumerate(rms_normalized.shape)]
+    pieces = lax.dynamic_update_slice_in_dim(
+        jnp.zeros(shape, rms_normalized.dtype), rms_normalized, here * step, axis=0
+    )
+    going_up = going_down = rms_normalized
+    for far in range(1, ways // 2 + 1):
+        going_up = lax.ppermute(going_up, "tensor", [(d, (d + 1) % ways) for d in range(ways)])
+        pieces = lax.dynamic_update_slice_in_dim(
+            pieces, going_up, (here - far) % ways * step, axis=0
+        )
+        if 2 * far < ways:
+            going_down = lax.ppermute(
+                going_down, "tensor", [(d, (d - 1) % ways) for d in range(ways)]
+            )
+            pieces = lax.dynamic_update_slice_in_dim(
+                pieces, going_down, (here + far) % ways * step, axis=0
+            )
     projected = jnp.concatenate(
         [
             jnp.dot(pieces, w_query, preferred_element_type=jnp.float32),

time: 282 us -> 292 us (1.035)
  starting transfers between devices: 0.04 us -> 27.2 us
  waiting for transfers between devices: 130 us -> 104 us
  local copies, waits for them, and re-layouts: 13.3 us -> 21.7 us
    all_gather x1 -> x0, waiting for transfers between devices: 60.4 us -> none  [body(): pieces = lax.all_gather(rms_normalized, 'tensor', axis=0, tiled=True)]
    ppermute x0 -> x7, starting transfers between devices: none -> 27.2 us  [the longest x4 16.2 us: body(): lax.ppermute(going_up, 'tensor', [(d, (d + 1) % ways) for d in range(ways)])]
    ppermute x0 -> x7, waiting for transfers between devices: none -> 24.2 us  [the longest x4 23.2 us: body(): lax.ppermute(going_up, 'tensor', [(d, (d + 1) % ways) for d in range(ways)])]
    all_gather x1, waiting for transfers between devices: 69.8 us -> 79.4 us  [sent_together(): filled = lax.all_gather(both, axis, axis=dim, tiled=True)]
    dynamic_update_slice x0 -> x7, local copies, waits for them, and re-layouts: none -> 5.93 us  [the longest x4 3.38 us: body(): lax.dynamic_update_slice_in_dim(pieces, going_up, (here - far) % ways * s...]
  transfers between devices with their start and end apart: 2 -> 8, of which waited for: 2 -> 7; matrix products, arithmetic and copies ran while one was open for 3% -> 5% of each run, Pallas kernels for 0% -> 0%
where the time goes in v1:
time: 292 us; the launch traced here: 291 us
  waiting for transfers between devices  104 us (36%)
  matrix products  98.8 us (34%)
  starting transfers between devices  27.2 us (9%)
  other arithmetic  23.5 us (8%)
  local copies, waits for them, and re-layouts  21.7 us (7%)
  between operations  15.5 us (5%)
    all_gather x1, waiting for transfers between devices, sent_together(): filled = lax.all_gather(both, axis, axis=dim, tiled=True)  79.4 us
    dot_general x16, matrix products, merge_block(): jnp.einsum('qkgd,skd->kgqs', query_heads, key_part, preferred_element_typ...  44.6 us
    dot_general x16, matrix products, merge_block(): jnp.einsum('kgqs,skd->kgqd', probs.astype(jnp.bfloat16), val_part, prefer...  43.3 us
    ppermute x4, waiting for transfers between devices, body(): lax.ppermute(going_up, 'tensor', [(d, (d + 1) % ways) for d in range(ways)])  23.2 us
    ppermute x4, starting transfers between devices, body(): lax.ppermute(going_up, 'tensor', [(d, (d + 1) % ways) for d in range(ways)])  16.2 us
    ppermute x3, starting transfers between devices, body(): lax.ppermute(going_down, 'tensor', [(d, (d - 1) % ways) for d in range(wa...  10.9 us
    reduce_sum x16, other arithmetic, merge_block(): totals = totals * rescale + jnp.sum(probs, -1)  9.2 us
    another operation x1, local copies, waits for them, and re-layouts  6.44 us
  transfers between devices with their start and end apart: 8, of which 7 were waited for; matrix products, arithmetic and copies ran while one was open for 5% of the time, Pallas kernels for 0%

profile of v1, /device:TPU:8, one launch (start us, length us, event | category | flops | bytes accessed | tf_op | source)
XLA Modules:
  0.0 291.4 jit_solution(17106018215552027897)
XLA Ops:
  6.5 0.8 convert_element_type.49
  7.4 1.2 fusion.23
  8.7 2.5 broadcast_in_dim.41
  11.1 1.2 constant_dynamic-update-slice_fusion.7
  12.3 3.5 %collective-permute-start = (bf16[64,4096]{1,0:T(8,128)(2,1)}, bf16[64,4096]{1,0:T(8,128)(2,1)S(1)}, u32[]{:S(2)}, u32[]{:S(2)}) collective-permute-start(bf16[64,4096]{1,0:T(8,128)(2,1)} %get-tuple-element.166), channel_id=1, source_target_pairs={{0,1},{1,2},{2,3},{3,4},{4,5},{5,6},{6,7},{7,0},{8,9},{9,10},{10,1... | collective-permute-start | bytes 1572872 | tf_op jit(solution)/shard_map/ppermute | solution.py:66
  15.9 6.1 %collective-permute-start.1 = (bf16[64,4096]{1,0:T(8,128)(2,1)}, bf16[64,4096]{1,0:T(8,128)(2,1)S(1)}, u32[]{:S(2)}, u32[]{:S(2)}) collective-permute-start(bf16[64,4096]{1,0:T(8,128)(2,1)} %get-tuple-element.166), channel_id=1, source_target_pairs={{0,7},{1,0},{2,1},{3,2},{4,3},{5,4},{6,5},{7,6},{8,15},{9,8},{10,9... | collective-permute-start | bytes 1572872 | tf_op jit(solution)/shard_map/ppermute | solution.py:71
  22.1 6.0 %collective-permute-done = bf16[64,4096]{1,0:T(8,128)(2,1)S(1)} collective-permute-done((bf16[64,4096]{1,0:T(8,128)(2,1)}, bf16[64,4096]{1,0:T(8,128)(2,1)S(1)}, u32[]{:S(2)}, u32[]{:S(2)}) %collective-permute-start) | collective-permute-done | bytes 524320 | tf_op jit(solution)/shard_map/ppermute | solution.py:66
  28.1 3.5 %collective-permute-start.2 = (bf16[64,4096]{1,0:T(8,128)(2,1)S(1)}, bf16[64,4096]{1,0:T(8,128)(2,1)S(1)}, u32[]{:S(2)}, u32[]{:S(2)}) collective-permute-start(bf16[64,4096]{1,0:T(8,128)(2,1)S(1)} %collective-permute-done), channel_id=1, source_target_pairs={{0,1},{1,2},{2,3},{3,4},{4,5},{5,6},{6,7},{7,0},{8,9},{9,10},{10,1... | collective-permute-start | bytes 1572872 | tf_op jit(solution)/shard_map/ppermute | solution.py:66
  31.6 2.8 collective-permute-start.3
  34.5 0.8 constant_dynamic-update-slice_fusion.6
  35.3 0.9 constant_dynamic-update-slice_fusion.5
  36.2 5.8 %collective-permute-done.2 = bf16[64,4096]{1,0:T(8,128)(2,1)S(1)} collective-permute-done((bf16[64,4096]{1,0:T(8,128)(2,1)S(1)}, bf16[64,4096]{1,0:T(8,128)(2,1)S(1)}, u32[]{:S(2)}, u32[]{:S(2)}) %collective-permute-start.2) | collective-permute-done | bytes 524320 | tf_op jit(solution)/shard_map/ppermute | solution.py:66
  42.0 4.3 %collective-permute-start.4 = (bf16[64,4096]{1,0:T(8,128)(2,1)S(1)}, bf16[64,4096]{1,0:T(8,128)(2,1)S(1)}, u32[]{:S(2)}, u32[]{:S(2)}) collective-permute-start(bf16[64,4096]{1,0:T(8,128)(2,1)S(1)} %collective-permute-done.2), channel_id=1, source_target_pairs={{0,1},{1,2},{2,3},{3,4},{4,5},{5,6},{6,7},{7,0},{8,9},{9,10},{10,1... | collective-permute-start | bytes 1572872 | tf_op jit(solution)/shard_map/ppermute | solution.py:66
  46.9 2.0 collective-permute-start.5
  48.9 0.9 constant_dynamic-update-slice_fusion.4
  49.7 0.8 constant_dynamic-update-slice_fusion.3
  50.6 5.1 %collective-permute-done.4 = bf16[64,4096]{1,0:T(8,128)(2,1)S(1)} collective-permute-done((bf16[64,4096]{1,0:T(8,128)(2,1)S(1)}, bf16[64,4096]{1,0:T(8,128)(2,1)S(1)}, u32[]{:S(2)}, u32[]{:S(2)}) %collective-permute-start.4) | collective-permute-done | bytes 524320 | tf_op jit(solution)/shard_map/ppermute | solution.py:66
  55.7 4.9 %collective-permute-start.6 = (bf16[64,4096]{1,0:T(8,128)(2,1)S(1)}, bf16[64,4096]{1,0:T(8,128)(2,1)S(1)}, u32[]{:S(2)}, u32[]{:S(2)}) collective-permute-start(bf16[64,4096]{1,0:T(8,128)(2,1)S(1)} %collective-permute-done.4), channel_id=1, source_target_pairs={{0,1},{1,2},{2,3},{3,4},{4,5},{5,6},{6,7},{7,0},{8,9},{9,10},{10,1... | collective-permute-start | bytes 1572872 | tf_op jit(solution)/shard_map/ppermute | solution.py:66
  60.6 0.8 constant_dynamic-update-slice_fusion.2
  61.8 0.8 constant_dynamic-update-slice_fusion.1
  62.7 6.4 %collective-permute-done.6 = bf16[64,4096]{1,0:T(8,128)(2,1)S(1)} collective-permute-done((bf16[64,4096]{1,0:T(8,128)(2,1)S(1)}, bf16[64,4096]{1,0:T(8,128)(2,1)S(1)}, u32[]{:S(2)}, u32[]{:S(2)}) %collective-permute-start.6) | collective-permute-done | bytes 524320 | tf_op jit(solution)/shard_map/ppermute | solution.py:66
  69.1 0.8 constant_dynamic-update-slice_fusion
  69.9 3.8 %convolution_bitcast_fusion.1 = f32[512,1,128]{0,2,1:T(8,128)S(1)} fusion(bf16[512,4096]{1,0:T(8,128)(2,1)} %constant_dynamic-update-slice_fusion, bf16[4096,128]{1,0:T(8,128)(2,1)S(1)} %copy-done.4), kind=kOutput, calls=%fused_computation.37 | convolution fusion | flops 536870912 | bytes 5505024 | tf_op jit(solution)/shard_map/dot_general | solution.py:80
  73.7 3.7 %convolution_convert_fusion = bf16[512,128]{0,1:T(8,128)(2,1)S(1)} fusion(bf16[512,4096]{1,0:T(8,128)(2,1)} %constant_dynamic-update-slice_fusion, bf16[4096,128]{1,0:T(8,128)(2,1)S(1)} %copy-done.3), kind=kOutput, calls=%fused_computation.38 | convolution fusion | flops 536936448 | bytes 5373952 | tf_op jit(solution)/shard_map/dot_general | solution.py:81
  82.5 1.9 multiply_cosine_fusion
  84.4 3.5 %fusion.45 = f32[512,256]{0,1:T(8,128)S(1)} fusion(bf16[512,4096]{1,0:T(8,128)(2,1)} %constant_dynamic-update-slice_fusion, bf16[4096,256]{1,0:T(8,128)(2,1)S(1)} %copy-done), kind=kOutput, calls=%fused_computation.81 | convolution fusion | flops 1073741824 | bytes 6815744 | tf_op jit(solution)/shard_map/dot_general | solution.py:79
  88.3 1.2 fusion.26
  89.6 79.4 %all-gather.2.cloned.1.call-done = bf16[8192,256]{0,1:T(8,128)(2,1)} async-done(((bf16[512,256]{0,1:T(8,128)(2,1)}), bf16[8192,256]{0,1:T(8,128)(2,1)}) %all-gather.2.cloned.1.call-update) | async-done | bytes 4194320 | tf_op jit(solution)/shard_map/all_gather | solution.py:13
  169.0 114.3 %conditional.1 = (f32[1,2,512]{2,1,0:T(2,128)S(1)}, f32[1,2,512,128]{3,2,1,0:T(8,128)S(1)}) conditional(s32[]{:T(128)} %convert_element_type.47, (bf16[8192,256]{0,1:T(8,128)(2,1)}, s32[8192]{0:T(1024)S(1)}, s32[16,512]{1,0:T(8,128)S(1)}, s32[16,512]{1,0:T(8,128)S(1)}, s32[512]{0:T(512)S(1)}, /*index=5*/s32[512]{0:T(512)S(1)}, ...), branch_computations={%region_3.8_spmd, %region_8.9_spmd} | conditional | flops 276453376 | bytes 34325800 | solution.py:149
  169.0 6.4 %copy.10 = bf16[8192,256]{1,0:T(8,128)(2,1)} copy(bf16[8192,256]{0,1:T(8,128)(2,1)} %get-tuple-element.134) | data formatting | bytes 8388608 | tf_op jit(solution)/shard_map
  175.4 4.5 %fusion.43 = (bf16[8192,128]{1,0:T(8,128)(2,1)}, bf16[8192,128]{1,0:T(8,128)(2,1)}) fusion(bf16[8192,256]{1,0:T(8,128)(2,1)} %copy.10), kind=kLoop, calls=%fused_computation.79 | loop fusion | bytes 8388608 | tf_op jit(solution)/shard_map/split | solution.py:14
  179.9 103.3 %while.14 = (s32[]{:T(128)}, f32[1,2,512]{2,1,0:T(2,128)S(1)}, f32[1,2,512]{2,1,0:T(2,128)S(1)}, f32[1,2,512,128]{3,2,1,0:T(8,128)S(1)}, s32[16,512]{1,0:T(8,128...) while((s32[]{:T(128)}, f32[1,2,512]{2,1,0:T(2,128)S(1)}, ...), condition=%wide.region_7.7_spmd.clone, body=%wide.region_4.6_spmd.clone.sunk | while | flops 276436992 | bytes 17384616 | solution.py:147
  180.3 2.8 fusion.60
  183.1 2.7 fusion.63
  186.7 2.8 fusion.60
  189.5 2.7 fusion.63
  193.2 2.8 fusion.60
  196.0 2.7 fusion.63
  199.6 2.8 fusion.60
  202.5 2.7 fusion.63
  206.1 2.8 fusion.60
  208.9 2.7 fusion.63
  212.6 2.8 fusion.60
  215.4 2.7 fusion.63
  219.0 2.8 fusion.60
  221.8 2.7 fusion.63
  225.5 2.8 fusion.60
  228.3 2.7 fusion.63
  231.9 2.8 fusion.60
  234.8 2.7 fusion.63
  238.4 2.8 fusion.60
  241.2 2.7 fusion.63
  244.9 2.8 fusion.60
  247.7 2.7 fusion.63
  251.3 2.8 fusion.60
  254.1 2.7 fusion.63
  257.8 2.8 fusion.60
  260.6 2.7 fusion.63
  264.2 2.8 fusion.60
  267.0 2.7 fusion.63
  270.7 2.8 fusion.60
  273.5 2.7 fusion.63
  277.1 2.8 fusion.60
  280.0 2.7 fusion.63
  (165 shorter events, 20.5 us)
Async XLA Ops:
  6.5 77.8 %copy-start = (bf16[4096,256]{1,0:T(8,128)(2,1)S(1)}, bf16[4096,256]{1,0:T(8,128)(2,1)}, u32[]{:S(2)}) copy-start(bf16[4096,256]{1,0:T(8,128)(2,1)} %param.12) | copy-start | bytes 6291460
  6.5 162.5 %all-gather.2.cloned.1.call-start = ((), (), s32[]{:S(2)}) async-start(), calls=%async_computation | async-start | bytes 4456448 | tf_op jit(solution)/shard_map/all_gather | solution.py:13
  8.6 2.5 copy-start.2
  12.3 15.8 %collective-permute-start = (bf16[64,4096]{1,0:T(8,128)(2,1)}, bf16[64,4096]{1,0:T(8,128)(2,1)S(1)}, u32[]{:S(2)}, u32[]{:S(2)}) collective-permute-start(bf16[64,4096]{1,0:T(8,128)(2,1)} %get-tuple-element.166), channel_id=1, source_target_pairs={{0,1},{1,2},{2,3},{3,4},{4,5},{5,6},{6,7},{7,0},{8,9},{9,10},{10,1... | collective-permute-start | bytes 1572872 | tf_op jit(solution)/shard_map/ppermute | solution.py:66
  15.9 15.8 %collective-permute-start.1 = (bf16[64,4096]{1,0:T(8,128)(2,1)}, bf16[64,4096]{1,0:T(8,128)(2,1)S(1)}, u32[]{:S(2)}, u32[]{:S(2)}) collective-permute-start(bf16[64,4096]{1,0:T(8,128)(2,1)} %get-tuple-element.166), channel_id=1, source_target_pairs={{0,7},{1,0},{2,1},{3,2},{4,3},{5,4},{6,5},{7,6},{8,15},{9,8},{10,9... | collective-permute-start | bytes 1572872 | tf_op jit(solution)/shard_map/ppermute | solution.py:71
  28.1 13.9 %collective-permute-start.2 = (bf16[64,4096]{1,0:T(8,128)(2,1)S(1)}, bf16[64,4096]{1,0:T(8,128)(2,1)S(1)}, u32[]{:S(2)}, u32[]{:S(2)}) collective-permute-start(bf16[64,4096]{1,0:T(8,128)(2,1)S(1)} %collective-permute-done), channel_id=1, source_target_pairs={{0,1},{1,2},{2,3},{3,4},{4,5},{5,6},{6,7},{7,0},{8,9},{9,10},{10,1... | collective-permute-start | bytes 1572872 | tf_op jit(solution)/shard_map/ppermute | solution.py:66
  31.6 15.2 %collective-permute-start.3 = (bf16[64,4096]{1,0:T(8,128)(2,1)S(1)}, bf16[64,4096]{1,0:T(8,128)(2,1)S(1)}, u32[]{:S(2)}, u32[]{:S(2)}) collective-permute-start(bf16[64,4096]{1,0:T(8,128)(2,1)S(1)} %collective-permute-done.1), channel_id=1, source_target_pairs={{0,7},{1,0},{2,1},{3,2},{4,3},{5,4},{6,5},{7,6},{8,15},{9,8},{10,9... | collective-permute-start | bytes 1572872 | tf_op jit(solution)/shard_map/ppermute | solution.py:71
  42.0 13.6 %collective-permute-start.4 = (bf16[64,4096]{1,0:T(8,128)(2,1)S(1)}, bf16[64,4096]{1,0:T(8,128)(2,1)S(1)}, u32[]{:S(2)}, u32[]{:S(2)}) collective-permute-start(bf16[64,4096]{1,0:T(8,128)(2,1)S(1)} %collective-permute-done.2), channel_id=1, source_target_pairs={{0,1},{1,2},{2,3},{3,4},{4,5},{5,6},{6,7},{7,0},{8,9},{9,10},{10,1... | collective-permute-start | bytes 1572872 | tf_op jit(solution)/shard_map/ppermute | solution.py:66
  46.9 15.0 %collective-permute-start.5 = (bf16[64,4096]{1,0:T(8,128)(2,1)S(1)}, bf16[64,4096]{1,0:T(8,128)(2,1)S(1)}, u32[]{:S(2)}, u32[]{:S(2)}) collective-permute-start(bf16[64,4096]{1,0:T(8,128)(2,1)S(1)} %collective-permute-done.3), channel_id=1, source_target_pairs={{0,7},{1,0},{2,1},{3,2},{4,3},{5,4},{6,5},{7,6},{8,15},{9,8},{10,9... | collective-permute-start | bytes 1572872 | tf_op jit(solution)/shard_map/ppermute | solution.py:71
  49.7 20.2 %copy-start.4 = (bf16[4096,128]{1,0:T(8,128)(2,1)S(1)}, bf16[4096,128]{1,0:T(8,128)(2,1)}, u32[]{:S(2)}) copy-start(bf16[4096,128]{1,0:T(8,128)(2,1)} %param.13) | copy-start | bytes 3145732
  55.7 13.4 %collective-permute-start.6 = (bf16[64,4096]{1,0:T(8,128)(2,1)S(1)}, bf16[64,4096]{1,0:T(8,128)(2,1)S(1)}, u32[]{:S(2)}, u32[]{:S(2)}) collective-permute-start(bf16[64,4096]{1,0:T(8,128)(2,1)S(1)} %collective-permute-done.4), channel_id=1, source_target_pairs={{0,1},{1,2},{2,3},{3,4},{4,5},{5,6},{6,7},{7,0},{8,9},{9,10},{10,1... | collective-permute-start | bytes 1572872 | tf_op jit(solution)/shard_map/ppermute | solution.py:66
  69.9 3.8 %copy-start.3 = (bf16[4096,128]{1,0:T(8,128)(2,1)S(1)}, bf16[4096,128]{1,0:T(8,128)(2,1)}, u32[]{:S(2)}) copy-start(bf16[4096,128]{1,0:T(8,128)(2,1)} %param.14) | copy-start | bytes 3145732
  73.7 5.7 %copy-start.5 = (s32[8192]{0:T(1024)S(1)}, s32[8192]{0:T(1024)}, u32[]{:S(2)}) copy-start(s32[8192]{0:T(1024)} %param.15) | copy-start | bytes 98308
  183.1 2.7 copy-start.1
  189.5 2.7 copy-start.1
  196.0 2.7 copy-start.1
  202.4 2.7 copy-start.1
  208.9 2.7 copy-start.1
  215.4 2.7 copy-start.1
  221.8 2.7 copy-start.1
  228.3 2.7 copy-start.1
  234.7 2.7 copy-start.1
  241.2 2.7 copy-start.1
  247.7 2.7 copy-start.1
  254.1 2.7 copy-start.1
  260.6 2.7 copy-start.1
  267.0 2.7 copy-start.1
  273.5 2.7 copy-start.1
  280.0 2.7 copy-start.1
Sparse Core Ops, SparseCore 0:
  78.8 90.1 all-gather.1
